TPU v7x, 512 devices: a whole 4x4x16 slice. The times are simulated.
512 devices in a mesh: blk: 16 (over x, z_hi, core), grp: 32 (over y, z_lo).
Axes of the slice: x: 4, y: 4, z: 16 (z_hi: 2, z_lo: 8; z = z_hi * 8 + z_lo), core: 2. Of those that a mesh axis runs over, the one named last changes fastest.
Arguments:
- blocks: float32 [1024, 4, 128, 128], P(('blk', 'grp')), may hold values from -1.5 to 1.5
- columns: int32 [1024, 4], P(('blk', 'grp')), may hold values from -1 to 1023, as said below
- owner_map: int32 [1024], P(('blk', 'grp')), may hold values from 0 to 1023, as said below
- targets: int32 [1024, 4], P(('blk', 'grp')), may hold values from 0 to 1023, as said below
Outputs:
- purified: float32 [1024, 4, 128, 128], P(('blk', 'grp'))
Inputs may be any that keep to these rules, and one draw needn't show every extreme that they name: `owner_map`: A permutation of the 1024 block rows; each row's multiply position lies in the same slab, on the same device of grp or on the one next to it; positions ((s * 32 + g) * 2 + i) belong to slab s, device g of grp, slot i. `columns`: live entries of a row are distinct, slot 0 is the row's own multiply position, and every live entry lies on the same grp index as the row's multiply position and at most 2 slabs away from it round the loop; empty slots are -1 and come last. `targets`: entries of a row are distinct, slot 0 is the row itself, all lie on the row's grp index and at most 2 slabs away round the loop.
All inputs are finite; a program needn't handle non-finite values.
Results may differ from a plain program's by a relative error of at most 0.0003.
Values sent between devices are 32-bit elements; how exact they have to be, the bound alone decides.
A program may use at most 64 MiB of HBM per device.

v0:
```python
import jax
import jax.numpy as jnp
from jax import lax
from jax.sharding import PartitionSpec as P

FULL_PRECISION = lax.Precision.HIGHEST


def from_behind(value, axis, by):
    peers = lax.axis_size(axis)
    return lax.ppermute(value, axis, [(i, (i + by) % peers) for i in range(peers)])


def padded(value, sides, width):
    for axis, dim in sides:
        peers, length = (lax.axis_size(axis), value.shape[dim])
        up = [(i, (i + 1) % peers) for i in range(peers - 1)]
        down = [(j, i) for i, j in up]
        last = lax.slice_in_dim(value, length - width, length, axis=dim)
        leading = lax.slice_in_dim(value, 0, width, axis=dim)
        before = lax.ppermute(last, axis, up)
        after = lax.ppermute(leading, axis, down)
        value = jnp.concatenate([before, value, after], axis=dim)
    return value


def pick_terms(left_blocks, left_cols, panel_blocks, panel_cols, panel_ids, wanted):
    matched = (left_cols[:, :, None] == panel_ids[None, None, :]).astype(jnp.float32)
    left_pick = jnp.einsum("iap,iaxy->ipxy", matched, left_blocks, precision=FULL_PRECISION)
    matched_right = (panel_cols[None, :, None, :] == wanted[:, None, :, None]).astype(jnp.float32)
    right_pick = jnp.einsum(
        "ipbc,pcxy->ipbxy", matched_right, panel_blocks, precision=FULL_PRECISION
    )
    return jnp.einsum("ipxz,ipbzy->ibxy", left_pick, right_pick, precision=FULL_PRECISION)


def travel(panel_data, reach_slabs):
    visits = []
    moving = from_behind((panel_data[0], panel_data[1]), "blk", -reach_slabs)
    visits.append((moving, reach_slabs))
    for step_index in range(1, 2 * reach_slabs + 1):
        moving = from_behind((moving[0], moving[1]), "blk", 1)
        visits.append((moving, reach_slabs - step_index))
    return visits


def per_device(blocks, columns, owner_map, targets):
    row_count = blocks.shape[0]
    block_order = blocks.shape[2]
    group_size = lax.axis_size("grp")
    slab_count = lax.axis_size("blk")
    reach_slabs = max(1, slab_count // 8)
    slab_index = lax.axis_index("blk")
    group_index = lax.axis_index("grp")
    slot_ids = jnp.arange(row_count, dtype=jnp.int32)
    own_ids = (slab_index * group_size + group_index) * row_count + slot_ids
    pattern = jnp.concatenate([(owner_map + 1)[:, None], columns], axis=1)
    wide_blocks, wide_pattern = (
        padded(blocks, (("grp", 0),), row_count),
        padded(pattern, (("grp", 0),), row_count),
    )
    chosen = wide_pattern[None, :, 0] == (own_ids + 1)[:, None]
    local_blocks = jnp.einsum(
        "sh,hkxy->skxy", chosen.astype(jnp.float32), wide_blocks, precision=FULL_PRECISION
    )
    local_cols = jnp.sum(
        jnp.where(chosen[:, :, None], wide_pattern[None, :, 1:], 0), axis=1
    ).astype(jnp.int32)

    def panel_ids(offset_slab):
        slab_at = jnp.mod(slab_index + offset_slab, slab_count)
        return (slab_at * group_size + group_index) * row_count + slot_ids

    first_visits = travel((local_blocks, local_cols), reach_slabs)
    square_blocks = jnp.zeros((row_count, targets.shape[1], block_order, block_order), jnp.float32)
    for visit_item in first_visits:
        panel_data, offset_slab = visit_item
        square_blocks = square_blocks + pick_terms(
            local_blocks, local_cols, panel_data[0], panel_data[1], panel_ids(offset_slab), targets
        )
    second_visits = travel((local_blocks, local_cols), reach_slabs)
    cube_blocks = jnp.zeros_like(square_blocks)
    for visit_item in second_visits:
        panel_data, offset_slab = visit_item
        cube_blocks = cube_blocks + pick_terms(
            square_blocks, targets, panel_data[0], panel_data[1], panel_ids(offset_slab), targets
        )
    return 3.0 * square_blocks - 2.0 * cube_blocks


def solution(mesh):
    return jax.shard_map(
        per_device,
        mesh=mesh,
        in_specs=(
            P(("blk", "grp"), None, None, None),
            P(("blk", "grp"), None),
            P(("blk", "grp")),
            P(("blk", "grp"), None),
        ),
        out_specs=P(("blk", "grp"), None, None, None),
        check_vma=False,
    )
```

profile of v0, /device:TPU:8, one launch (start us, length us, event | category | flops | bytes accessed | tf_op | source)
XLA Modules:
  0.0 297.3 jit_solution(8741095677091959084)
XLA Ops:
  1.5 13.0 %collective-permute-start.1 = (s32[2,5]{1,0:T(2,128)S(1)}, s32[2,5]{1,0:T(2,128)S(1)}, u32[]{:S(2)}, u32[]{:S(2)}) collective-permute-start(s32[2,5]{1,0:T(2,128)S(1)} %pad_add_fusion.1), channel_id=1, source_target_pairs={{1,0},{2,1},{3,2},{4,3},{5,4},{6,5},{7,6},{8,7},{9,8},{10,9},{11,1... | collective-permute-start | bytes 128 | tf_op jit(solution)/shard_map/ppermute | solution.py:22
  17.9 11.4 %collective-permute-start.3 = (f32[2,4,128,128]{3,0,2,1:T(2,128)S(1)}, f32[2,4,128,128]{3,0,2,1:T(2,128)S(1)}, u32[]{:S(2)}, u32[]{:S(2)}) collective-permute-start(f32[2,4,128,128]{3,0,2,1:T(2,128)S(1)} %copy.46), channel_id=1, source_target_pairs={{1,0},{2,1},{3,2},{4,3},{5,4},{6,5},{7,6},{8,7},{9,8},{10,9},{11,1... | collective-permute-start | bytes 1572872 | tf_op jit(solution)/shard_map/ppermute | solution.py:22
  31.7 10.0 %collective-permute-done.3 = f32[2,4,128,128]{3,0,2,1:T(2,128)S(1)} collective-permute-done((f32[2,4,128,128]{3,0,2,1:T(2,128)S(1)}, f32[2,4,128,128]{3,0,2,1:T(2,128)S(1)}, u32[]{:S(2)}, u32[]{:S(2)}) %collective-permute-start.3) | collective-permute-done | bytes 524320 | tf_op jit(solution)/shard_map/ppermute | solution.py:22
  41.7 14.0 %collective-permute-done.2 = f32[2,4,128,128]{3,0,2,1:T(2,128)S(1)} collective-permute-done((f32[2,4,128,128]{3,0,2,1:T(2,128)S(1)}, f32[2,4,128,128]{3,0,2,1:T(2,128)S(1)}, u32[]{:S(2)}, u32[]{:S(2)}) %collective-permute-start.2) | collective-permute-done | bytes 524320 | tf_op jit(solution)/shard_map/ppermute | solution.py:21
  57.4 10.2 %collective-permute-start.4 = (f32[2,4,128,128]{3,0,2,1:T(2,128)S(1)}, f32[2,4,128,128]{3,0,2,1:T(2,128)S(1)}, u32[]{:S(2)}, u32[]{:S(2)}) collective-permute-start(f32[2,4,128,128]{3,0,2,1:T(2,128)S(1)} %fusion), channel_id=1, source_target_pairs={{0,448},{32,480},{64,0},{96,32},{128,64},{160,96},{192,128},{224,1... | collective-permute-start | bytes 1572872 | tf_op jit(solution)/shard_map/ppermute | solution.py:11
  67.9 41.9 %collective-permute-done.4 = f32[2,4,128,128]{3,0,2,1:T(2,128)S(1)} collective-permute-done((f32[2,4,128,128]{3,0,2,1:T(2,128)S(1)}, f32[2,4,128,128]{3,0,2,1:T(2,128)S(1)}, u32[]{:S(2)}, u32[]{:S(2)}) %collective-permute-start.4) | collective-permute-done | bytes 524320 | tf_op jit(solution)/shard_map/ppermute | solution.py:11
  111.8 4.4 %collective-permute-start.5 = (s32[2,4]{1,0:T(2,128)S(1)}, s32[2,4]{1,0:T(2,128)S(1)}, u32[]{:S(2)}, u32[]{:S(2)}) collective-permute-start(s32[2,4]{1,0:T(2,128)S(1)} %select_reduce_fusion), channel_id=1, source_target_pairs={{0,448},{32,480},{64,0},{96,32},{128,64},{160,96},{192,128},{224,1... | collective-permute-start | bytes 104 | tf_op jit(solution)/shard_map/ppermute | solution.py:11
  116.3 10.0 %collective-permute-done.5 = s32[2,4]{1,0:T(2,128)S(1)} collective-permute-done((s32[2,4]{1,0:T(2,128)S(1)}, s32[2,4]{1,0:T(2,128)S(1)}, u32[]{:S(2)}, u32[]{:S(2)}) %collective-permute-start.5) | collective-permute-done | bytes 64 | tf_op jit(solution)/shard_map/ppermute | solution.py:11
  126.2 5.7 %collective-permute-start.7 = (s32[2,4]{1,0:T(2,128)S(1)}, s32[2,4]{1,0:T(2,128)S(1)}, u32[]{:S(2)}, u32[]{:S(2)}) collective-permute-start(s32[2,4]{1,0:T(2,128)S(1)} %collective-permute-done.5), channel_id=1, source_target_pairs={{0,32},{32,64},{64,96},{96,128},{128,160},{160,192},{192,224},{224... | collective-permute-start | bytes 104 | tf_op jit(solution)/shard_map/ppermute | solution.py:11
  132.0 13.1 %collective-permute-done.7 = s32[2,4]{1,0:T(2,128)S(1)} collective-permute-done((s32[2,4]{1,0:T(2,128)S(1)}, s32[2,4]{1,0:T(2,128)S(1)}, u32[]{:S(2)}, u32[]{:S(2)}) %collective-permute-start.7) | collective-permute-done | bytes 64 | tf_op jit(solution)/shard_map/ppermute | solution.py:11
  147.0 13.8 %collective-permute-done.9 = s32[2,4]{1,0:T(2,128)S(1)} collective-permute-done((s32[2,4]{1,0:T(2,128)S(1)}, s32[2,4]{1,0:T(2,128)S(1)}, u32[]{:S(2)}, u32[]{:S(2)}) %collective-permute-start.9) | collective-permute-done | bytes 64 | tf_op jit(solution)/shard_map/ppermute | solution.py:11
  162.7 13.8 %collective-permute-done.11 = s32[2,4]{1,0:T(2,128)S(1)} collective-permute-done((s32[2,4]{1,0:T(2,128)S(1)}, s32[2,4]{1,0:T(2,128)S(1)}, u32[]{:S(2)}, u32[]{:S(2)}) %collective-permute-start.11) | collective-permute-done | bytes 64 | tf_op jit(solution)/shard_map/ppermute | solution.py:11
  189.7 31.0 %collective-permute-done.8 = f32[2,4,128,128]{3,0,2,1:T(2,128)} collective-permute-done((f32[2,4,128,128]{3,0,2,1:T(2,128)S(1)}, f32[2,4,128,128]{3,0,2,1:T(2,128)}, u32[]{:S(2)}, u32[]{:S(2)}) %collective-permute-start.8) | collective-permute-done | bytes 524320 | tf_op jit(solution)/shard_map/ppermute | solution.py:11
  222.8 2.2 convolution_bitcast_fusion.3
  227.4 2.2 convolution_bitcast_fusion.2
  230.0 24.9 %collective-permute-done.10 = f32[2,4,128,128]{3,0,2,1:T(2,128)} collective-permute-done((f32[2,4,128,128]{3,0,2,1:T(2,128)}, f32[2,4,128,128]{3,0,2,1:T(2,128)}, u32[]{:S(2)}, u32[]{:S(2)}) %collective-permute-start.10) | collective-permute-done | bytes 524320 | tf_op jit(solution)/shard_map/ppermute | solution.py:11
  256.8 2.8 convolution_bitcast_fusion.12
  259.6 3.2 %convolution_bitcast_fusion.1 = f32[2,2,4,128,128]{4,2,0,3,1:T(4,128)} fusion(f32[2,4,128,128,1]{3,0,2,1,4:T(2,128)} %bitcast.30, s32[2,4]{1,0:T(2,128)S(1)} %collective-permute-done.11, s32[2,4]{1,0:T(2,128)S(1)} %copy-done.8), kind=kOutput, calls=%fused_computation.7 | convolution fusion | flops 12582976 | bytes 1572928 | tf_op jit(solution)/shard_map/ipbc,pcxy->ipbxy/dot_general | solution.py:31
  264.4 3.0 convolution_bitcast_fusion.11
  267.4 9.2 %collective-permute-done.12 = f32[2,4,128,128]{3,0,2,1:T(2,128)} collective-permute-done((f32[2,4,128,128]{3,0,2,1:T(2,128)}, f32[2,4,128,128]{3,0,2,1:T(2,128)}, u32[]{:S(2)}, u32[]{:S(2)}) %collective-permute-start.12) | collective-permute-done | bytes 524320 | tf_op jit(solution)/shard_map/ppermute | solution.py:11
  276.5 3.2 %convolution_bitcast_fusion = f32[2,2,4,128,128]{4,2,0,3,1:T(4,128)} fusion(f32[2,4,128,128,1]{3,0,2,1,4:T(2,128)} %bitcast.39, s32[2,4]{1,0:T(2,128)S(1)} %collective-permute-done.13, s32[2,4]{1,0:T(2,128)S(1)} %copy-done.8), kind=kOutput, calls=%fused_computation.6 | convolution fusion | flops 12582976 | bytes 1572928 | tf_op jit(solution)/shard_map/ipbc,pcxy->ipbxy/dot_general | solution.py:31
  279.8 2.5 copy.68
  282.3 2.4 convolution_bitcast_fusion.10
  284.7 2.2 fusion.10
  (73 shorter events, 46.7 us)
Async XLA Ops:
  0.0 31.4 %copy-start.9 = (s32[2,4]{1,0:T(2,128)S(1)}, s32[2,4]{1,0:T(2,128)}, u32[]{:S(2)}) copy-start(s32[2,4]{1,0:T(2,128)} %param.5) | copy-start | bytes 100
  1.5 29.9 %collective-permute-start.1 = (s32[2,5]{1,0:T(2,128)S(1)}, s32[2,5]{1,0:T(2,128)S(1)}, u32[]{:S(2)}, u32[]{:S(2)}) collective-permute-start(s32[2,5]{1,0:T(2,128)S(1)} %pad_add_fusion.1), channel_id=1, source_target_pairs={{1,0},{2,1},{3,2},{4,3},{5,4},{6,5},{7,6},{8,7},{9,8},{10,9},{11,1... | collective-permute-start | bytes 128 | tf_op jit(solution)/shard_map/ppermute | solution.py:22
  14.6 16.8 %collective-permute-start = (s32[2,5]{1,0:T(2,128)S(1)}, s32[2,5]{1,0:T(2,128)S(1)}, u32[]{:S(2)}, u32[]{:S(2)}) collective-permute-start(s32[2,5]{1,0:T(2,128)S(1)} %pad_add_fusion.1), channel_id=1, source_target_pairs={{0,1},{1,2},{2,3},{3,4},{4,5},{5,6},{6,7},{7,8},{8,9},{9,10},{10,1... | collective-permute-start | bytes 128 | tf_op jit(solution)/shard_map/ppermute | solution.py:21
  17.9 23.8 %collective-permute-start.3 = (f32[2,4,128,128]{3,0,2,1:T(2,128)S(1)}, f32[2,4,128,128]{3,0,2,1:T(2,128)S(1)}, u32[]{:S(2)}, u32[]{:S(2)}) collective-permute-start(f32[2,4,128,128]{3,0,2,1:T(2,128)S(1)} %copy.46), channel_id=1, source_target_pairs={{1,0},{2,1},{3,2},{4,3},{5,4},{6,5},{7,6},{8,7},{9,8},{10,9},{11,1... | collective-permute-start | bytes 1572872 | tf_op jit(solution)/shard_map/ppermute | solution.py:22
  29.4 26.3 %collective-permute-start.2 = (f32[2,4,128,128]{3,0,2,1:T(2,128)S(1)}, f32[2,4,128,128]{3,0,2,1:T(2,128)S(1)}, u32[]{:S(2)}, u32[]{:S(2)}) collective-permute-start(f32[2,4,128,128]{3,0,2,1:T(2,128)S(1)} %copy.46), channel_id=1, source_target_pairs={{0,1},{1,2},{2,3},{3,4},{4,5},{5,6},{6,7},{7,8},{8,9},{9,10},{10,1... | collective-permute-start | bytes 1572872 | tf_op jit(solution)/shard_map/ppermute | solution.py:21
  57.4 52.4 %collective-permute-start.4 = (f32[2,4,128,128]{3,0,2,1:T(2,128)S(1)}, f32[2,4,128,128]{3,0,2,1:T(2,128)S(1)}, u32[]{:S(2)}, u32[]{:S(2)}) collective-permute-start(f32[2,4,128,128]{3,0,2,1:T(2,128)S(1)} %fusion), channel_id=1, source_target_pairs={{0,448},{32,480},{64,0},{96,32},{128,64},{160,96},{192,128},{224,1... | collective-permute-start | bytes 1572872 | tf_op jit(solution)/shard_map/ppermute | solution.py:11
  109.8 72.7 %collective-permute-start.6 = (f32[2,4,128,128]{3,0,2,1:T(2,128)S(1)}, f32[2,4,128,128]{3,0,2,1:T(2,128)S(1)}, u32[]{:S(2)}, u32[]{:S(2)}) collective-permute-start(f32[2,4,128,128]{3,0,2,1:T(2,128)S(1)} %collective-permute-done.4), channel_id=1, source_target_pairs={{0,32},{32,64},{64,96},{96,128},{128,160},{160,192},{192,224},{224... | collective-permute-start | bytes 1572872 | tf_op jit(solution)/shard_map/ppermute | solution.py:11
  111.8 14.4 %collective-permute-start.5 = (s32[2,4]{1,0:T(2,128)S(1)}, s32[2,4]{1,0:T(2,128)S(1)}, u32[]{:S(2)}, u32[]{:S(2)}) collective-permute-start(s32[2,4]{1,0:T(2,128)S(1)} %select_reduce_fusion), channel_id=1, source_target_pairs={{0,448},{32,480},{64,0},{96,32},{128,64},{160,96},{192,128},{224,1... | collective-permute-start | bytes 104 | tf_op jit(solution)/shard_map/ppermute | solution.py:11
  126.2 18.8 %collective-permute-start.7 = (s32[2,4]{1,0:T(2,128)S(1)}, s32[2,4]{1,0:T(2,128)S(1)}, u32[]{:S(2)}, u32[]{:S(2)}) collective-permute-start(s32[2,4]{1,0:T(2,128)S(1)} %collective-permute-done.5), channel_id=1, source_target_pairs={{0,32},{32,64},{64,96},{96,128},{128,160},{160,192},{192,224},{224... | collective-permute-start | bytes 104 | tf_op jit(solution)/shard_map/ppermute | solution.py:11
  145.0 15.7 %collective-permute-start.9 = (s32[2,4]{1,0:T(2,128)S(1)}, s32[2,4]{1,0:T(2,128)S(1)}, u32[]{:S(2)}, u32[]{:S(2)}) collective-permute-start(s32[2,4]{1,0:T(2,128)S(1)} %collective-permute-done.7), channel_id=1, source_target_pairs={{0,32},{32,64},{64,96},{96,128},{128,160},{160,192},{192,224},{224... | collective-permute-start | bytes 104 | tf_op jit(solution)/shard_map/ppermute | solution.py:11
  160.7 15.7 %collective-permute-start.11 = (s32[2,4]{1,0:T(2,128)S(1)}, s32[2,4]{1,0:T(2,128)S(1)}, u32[]{:S(2)}, u32[]{:S(2)}) collective-permute-start(s32[2,4]{1,0:T(2,128)S(1)} %collective-permute-done.9), channel_id=1, source_target_pairs={{0,32},{32,64},{64,96},{96,128},{128,160},{160,192},{192,224},{224... | collective-permute-start | bytes 104 | tf_op jit(solution)/shard_map/ppermute | solution.py:11
  176.5 90.9 %collective-permute-start.13 = (s32[2,4]{1,0:T(2,128)S(1)}, s32[2,4]{1,0:T(2,128)S(1)}, u32[]{:S(2)}, u32[]{:S(2)}) collective-permute-start(s32[2,4]{1,0:T(2,128)S(1)} %collective-permute-done.11), channel_id=1, source_target_pairs={{0,32},{32,64},{64,96},{96,128},{128,160},{160,192},{192,224},{224... | collective-permute-start | bytes 104 | tf_op jit(solution)/shard_map/ppermute | solution.py:11
  180.9 6.2 %copy-start.8 = (s32[2,4]{1,0:T(2,128)S(1)}, s32[2,4]{1,0:T(2,128)}, u32[]{:S(2)}) copy-start(s32[2,4]{1,0:T(2,128)} %param.7) | copy-start | bytes 100
  182.5 5.7 %copy-start.7 = (f32[2,4,128,128]{3,0,2,1:T(2,128)}, f32[2,4,128,128]{3,0,2,1:T(2,128)S(1)}, u32[]{:S(2)}) copy-start(f32[2,4,128,128]{3,0,2,1:T(2,128)S(1)} %collective-permute-done.6) | copy-start | bytes 1572868
  182.5 38.2 %collective-permute-start.8 = (f32[2,4,128,128]{3,0,2,1:T(2,128)S(1)}, f32[2,4,128,128]{3,0,2,1:T(2,128)}, u32[]{:S(2)}, u32[]{:S(2)}) collective-permute-start(f32[2,4,128,128]{3,0,2,1:T(2,128)S(1)} %collective-permute-done.6), channel_id=1, source_target_pairs={{0,32},{32,64},{64,96},{96,128},{128,160},{160,192},{192,224},{224... | collective-permute-start | bytes 1572872 | tf_op jit(solution)/shard_map/ppermute | solution.py:11
  220.7 34.2 %collective-permute-start.10 = (f32[2,4,128,128]{3,0,2,1:T(2,128)}, f32[2,4,128,128]{3,0,2,1:T(2,128)}, u32[]{:S(2)}, u32[]{:S(2)}) collective-permute-start(f32[2,4,128,128]{3,0,2,1:T(2,128)} %collective-permute-done.8), channel_id=1, source_target_pairs={{0,32},{32,64},{64,96},{96,128},{128,160},{160,192},{192,224},{224... | collective-permute-start | bytes 1572872 | tf_op jit(solution)/shard_map/ppermute | solution.py:11
  254.9 21.6 %collective-permute-start.12 = (f32[2,4,128,128]{3,0,2,1:T(2,128)}, f32[2,4,128,128]{3,0,2,1:T(2,128)}, u32[]{:S(2)}, u32[]{:S(2)}) collective-permute-start(f32[2,4,128,128]{3,0,2,1:T(2,128)} %collective-permute-done.10), channel_id=1, source_target_pairs={{0,32},{32,64},{64,96},{96,128},{128,160},{160,192},{192,224},{224... | collective-permute-start | bytes 1572872 | tf_op jit(solution)/shard_map/ppermute | solution.py:11
  264.4 15.4 %copy-start = (f32[2,2,4,128,128]{3,4,1,2,0:T(8,128)}, f32[2,2,4,128,128]{3,4,1,2,0:T(8,128)S(1)}, u32[]{:S(2)}) copy-start(f32[2,2,4,128,128]{3,4,1,2,0:T(8,128)S(1)} %copy.64) | copy-start | bytes 3145732
  282.3 2.4 copy-start.3
  282.3 2.4 copy-start.5
  282.3 2.4 copy-start.6
  288.5 1.9 copy-start.2
  290.4 1.2 copy-start.1
  294.0 1.2 copy-start.4
where the time goes:
time: 298 us; the launch traced here: 297 us
  waiting for transfers between devices  182 us (61%)
  starting transfers between devices  62.3 us (21%)
  matrix products  41.2 us (14%)
  local copies, waits for them, and re-layouts  9.95 us (3%)
    ppermute x10, waiting for transfers between devices, from_behind(): lax.ppermute(value, axis, [(i, (i + by) % peers) for i in range(peers)])  158 us
    ppermute x10, starting transfers between devices, from_behind(): lax.ppermute(value, axis, [(i, (i + by) % peers) for i in range(peers)])  34 us
    ppermute x2, starting transfers between devices, padded(): after = lax.ppermute(leading, axis, down)  24.5 us
    dot_general x10, matrix products, pick_terms(): jnp.einsum('ipxz,ipbzy->ibxy', left_pick, right_pick, precision=FULL_PREC...  17.7 us
    ppermute x2, waiting for transfers between devices, padded(): before = lax.ppermute(last, axis, up)  14 us
    dot_general x5, matrix products, pick_terms(): jnp.einsum('ipbc,pcxy->ipbxy', matched_right, panel_blocks, precision=FUL...  12 us
    ppermute x2, waiting for transfers between devices, padded(): after = lax.ppermute(leading, axis, down)  10 us
    dot_general x10, matrix products, pick_terms(): jnp.einsum('iap,iaxy->ipxy', matched, left_blocks, precision=FULL_PRECISION)  9.84 us
  transfers between devices with their start and end apart: 14, of which 10 were waited for; matrix products, arithmetic and copies ran while one was open for 10% of the time, Pallas kernels for 0%

commit v1 on v0

v1 whole, which is shorter than its diff:
```python
import functools

import jax
import jax.numpy as jnp
from jax import lax
from jax.experimental import pallas as pl
from jax.experimental.pallas import tpu as pltpu
from jax.sharding import PartitionSpec as P

MESH = pl.DeviceIdType.MESH
ROWS, SLOTS, ORDER = 2, 4, 128
CHUNKS = ROWS * SLOTS
Z_LO = 8


def place():
    slab, group = lax.axis_index("blk"), lax.axis_index("grp")
    return slab // 4, (slab // 2) % 2, slab % 2, group // Z_LO, group % Z_LO


def exchange_kernel(
    blocks, pattern, far, far_pattern, mid, mid_pattern, send_sem, recv_sem
):
    x, z_hi, core, y, z_lo = place()
    half = z_lo // 4

    def at(x_, hi_, core_, lo_):
        return ((x_ * 2 + hi_) * 2 + core_, y * Z_LO + lo_)

    up = at(x, (z_hi + half) % 2, core, (z_lo + 4) % Z_LO)
    down = at(x, (z_hi + half + 1) % 2, core, (z_lo + 4) % Z_LO)
    x_to = at((x + 5 - 2 * z_hi) % 4, z_hi, core, z_lo)
    x_from = at((x + 3 + 2 * z_hi) % 4, z_hi, core, z_lo)
    sibling = at(x, z_hi, 1 - core, z_lo)

    barrier = pltpu.get_barrier_semaphore()
    for peer in (up, down, x_to, x_from, sibling):
        pl.semaphore_signal(barrier, inc=1, device_id=peer, device_id_type=MESH)
    pl.semaphore_wait(barrier, 5)

    def copy(stage, i, src, dst, peer):
        return pltpu.make_async_remote_copy(
            src_ref=src,
            dst_ref=dst,
            send_sem=send_sem.at[stage, i],
            recv_sem=recv_sem.at[stage, i],
            device_id=peer,
            device_id_type=MESH,
        )

    pieces = [CHUNKS] + [c for i in range(CHUNKS // 2) for c in (i, i + CHUNKS // 2)]

    def heading(i):
        return up if i < CHUNKS // 2 or i == CHUNKS else down

    def own(i):
        return pattern if i == CHUNKS else blocks.at[i]

    def middle(i):
        return mid_pattern if i == CHUNKS else mid.at[i]

    def slot(k, i):
        return far_pattern.at[k] if i == CHUNKS else far.at[k, i]

    first = {i: copy(0, i, own(i), middle(i), heading(i)) for i in pieces}
    second = {i: copy(1, i, middle(i), slot(0, i), heading(i)) for i in pieces}
    across = {i: copy(2, i, slot(0, i), slot(1, i), x_to) for i in pieces}
    beside = {i: copy(3, i, own(i), slot(2, i), sibling) for i in pieces}
    source = (z_hi + core) % 2
    last = {i: copy(4, i, slot(source, i), slot(3, i), sibling) for i in pieces}

    for i in pieces:
        first[i].start()
    for i in pieces:
        beside[i].start()
    for i in pieces:
        first[i].wait_recv()
        second[i].start()
    for i in pieces:
        second[i].wait_recv()
        across[i].start()
    for i in pieces:
        across[i].wait_recv()
        last[i].start()
    for i in pieces:
        beside[i].wait_recv()
        last[i].wait_recv()
    for stage in (first, second, across, beside, last):
        for i in pieces:
            stage[i].wait_send()


def exchange(blocks, pattern):
    vmem = pl.BlockSpec(memory_space=pltpu.VMEM)
    return pl.pallas_call(
        exchange_kernel,
        out_shape=(
            jax.ShapeDtypeStruct((4, CHUNKS, ORDER, ORDER), jnp.float32),
            jax.ShapeDtypeStruct((4, 8, 128), jnp.int32),
        ),
        in_specs=[vmem, vmem],
        out_specs=(vmem, vmem),
        scratch_shapes=[
            pltpu.VMEM((CHUNKS, ORDER, ORDER), jnp.float32),
            pltpu.VMEM((8, 128), jnp.int32),
            pltpu.SemaphoreType.DMA((5, CHUNKS + 1)),
            pltpu.SemaphoreType.DMA((5, CHUNKS + 1)),
        ],
        compiler_params=pltpu.CompilerParams(collective_id=0, has_side_effects=True),
        name="exchange",
    )(blocks, pattern)


PANEL = 5 * CHUNKS


def split(value):
    high = value.astype(jnp.bfloat16)
    return high, (value - high.astype(jnp.float32)).astype(jnp.bfloat16)


def dot3(left, right_high, right_low):
    high, low = split(left)
    dot = functools.partial(jnp.dot, preferred_element_type=jnp.float32)
    return dot(high, right_high) + (dot(high, right_low) + dot(low, right_high))


def purify_kernel(index, own, far, out, panel_high, panel_low, right_high, right_low):
    def fill(i, value):
        high, low = split(value)
        panel_high[i] = high
        panel_low[i] = low

    for i in range(CHUNKS):
        fill(i, own[i])

    @pl.loop(0, 4 * CHUNKS)
    def _(i):
        fill(CHUNKS + i, far[i])

    panel_high[PANEL] = jnp.zeros((ORDER, ORDER), jnp.bfloat16)
    panel_low[PANEL] = jnp.zeros((ORDER, ORDER), jnp.bfloat16)

    def product(stage, j, left):
        for a in range(SLOTS):
            for b in range(SLOTS):
                at = index[((stage * ROWS + j) * SLOTS + a) * SLOTS + b]
                rows, cols = pl.ds(a * ORDER, ORDER), pl.ds(b * ORDER, ORDER)
                right_high[rows, cols] = panel_high[at]
                right_low[rows, cols] = panel_low[at]
        return dot3(left, right_high[...], right_low[...])

    for j in range(ROWS):
        left = jnp.concatenate([own[j * SLOTS + a] for a in range(SLOTS)], axis=1)
        square = product(0, j, left)
        cube = product(1, j, square)
        result = 3.0 * square - 2.0 * cube
        for b in range(SLOTS):
            out[j, b] = result[:, b * ORDER : (b + 1) * ORDER]


def purify(index, own, far):
    vmem = pl.BlockSpec(memory_space=pltpu.VMEM)
    return pl.pallas_call(
        purify_kernel,
        out_shape=jax.ShapeDtypeStruct((ROWS, SLOTS, ORDER, ORDER), jnp.float32),
        in_specs=[pl.BlockSpec(memory_space=pltpu.SMEM), vmem, vmem],
        out_specs=vmem,
        scratch_shapes=[
            pltpu.VMEM((PANEL + 1, ORDER, ORDER), jnp.bfloat16),
            pltpu.VMEM((PANEL + 1, ORDER, ORDER), jnp.bfloat16),
            pltpu.VMEM((SLOTS * ORDER, SLOTS * ORDER), jnp.bfloat16),
            pltpu.VMEM((SLOTS * ORDER, SLOTS * ORDER), jnp.bfloat16),
        ],
        name="purify",
    )(index, own, far)


def from_neighbours(value, axis):
    peers = lax.axis_size(axis)
    up = [(i, i + 1) for i in range(peers - 1)]
    down = [(i + 1, i) for i in range(peers - 1)]
    return lax.ppermute(value, axis, up), lax.ppermute(value, axis, down)


def per_device(blocks, columns, owner_map, targets):
    group_size, slab_count = lax.axis_size("grp"), lax.axis_size("blk")
    slab, group = lax.axis_index("blk"), lax.axis_index("grp")
    _, z_hi, core, _, _ = place()
    slot_ids = jnp.arange(ROWS, dtype=jnp.int32)

    labels = jnp.concatenate([(owner_map + 1)[:, None], columns], axis=1)
    below, above = from_neighbours(blocks, "grp")
    labels_below, labels_above = from_neighbours(labels, "grp")
    wide_labels = jnp.concatenate([labels_below, labels, labels_above], axis=0)
    own_ids = (slab * group_size + group) * ROWS + slot_ids
    chosen = wide_labels[None, :, 0] == (own_ids + 1)[:, None]
    rows = [value[i] for value in (below, blocks, above) for i in range(ROWS)]
    local = jnp.stack(
        [
            sum(jnp.where(chosen[j, h], rows[h], 0.0) for h in range(3 * ROWS))
            for j in range(ROWS)
        ]
    ).reshape(CHUNKS, ORDER, ORDER)
    local_cols = jnp.sum(
        jnp.where(chosen[:, :, None], wide_labels[None, :, 1:], 0), axis=1
    ).astype(jnp.int32)

    pattern = jnp.pad(local_cols, ((0, 8 - ROWS), (0, 128 - SLOTS)))
    far, far_pattern = exchange(local, pattern)

    two, one = 2 - 4 * z_hi, 1 - 2 * core
    offsets = jnp.stack([jnp.zeros_like(two), two, -two, one, -one])
    ids = (jnp.mod(slab + offsets, slab_count) * group_size + group) * ROWS
    row_ids = (ids[:, None] + slot_ids[None, :]).reshape(-1)
    cols = jnp.concatenate([local_cols[None], far_pattern[:, :ROWS, :SLOTS]], axis=0)
    cols = cols.reshape(PANEL)
    block_rows = jnp.repeat(row_ids, SLOTS)
    left_ids = jnp.stack([local_cols, targets])
    found = (left_ids[:, :, :, None, None] == block_rows) & (
        targets[None, :, None, :, None] == cols
    )
    index = jnp.min(
        jnp.where(found, jnp.arange(PANEL, dtype=jnp.int32), PANEL), axis=-1
    ).reshape(-1)
    return purify(index, local, far.reshape(4 * CHUNKS, ORDER, ORDER))


def solution(mesh):
    return jax.shard_map(
        per_device,
        mesh=mesh,
        in_specs=(
            P(("blk", "grp"), None, None, None),
            P(("blk", "grp"), None),
            P(("blk", "grp")),
            P(("blk", "grp"), None),
        ),
        out_specs=P(("blk", "grp"), None, None, None),
        check_vma=False,
    )
```

time: 298 us -> 129 us (0.43)
  the two profiles are of different devices: /device:TPU:8 before, /device:TPU:49 now
where the time goes in v1:
time: 129 us
  Pallas kernels  75.8 us (59%)
  starting transfers between devices  18.3 us (14%)
  waiting for transfers between devices  18 us (14%)
  other arithmetic  13.3 us (10%)
  local copies, waits for them, and re-layouts  3.43 us (3%)
    pallas_call x1, Pallas kernels, exchange(): pl.pallas_call(exchange_kernel, out_shape=(jax.ShapeDtypeStruct((4, CHUNK...  70.8 us
    ppermute x4, starting transfers between devices, from_neighbours(): return (lax.ppermute(value, axis, up), lax.ppermute(value, axis, down))  18.3 us
    ppermute x4, waiting for transfers between devices, from_neighbours(): return (lax.ppermute(value, axis, up), lax.ppermute(value, axis, down))  18 us
    add x2, other arithmetic, per_device(): sum((jnp.where(chosen[j, h], rows[h], 0.0) for h in range(3 * ROWS)))  8.71 us
    pallas_call x1, Pallas kernels, purify(): pl.pallas_call(purify_kernel, out_shape=jax.ShapeDtypeStruct((ROWS, SLOTS...  4.99 us
  transfers between devices with their start and end apart: 4, of which 2 were waited for; matrix products, arithmetic and copies ran while one was open for 3% of the time, Pallas kernels for 0%

profile of v1, /device:TPU:49, one launch (start us, length us, event | category | flops | bytes accessed | tf_op | source)
XLA Modules:
  0.0 129.0 jit_solution(4424736379855247430)
XLA Ops:
  0.0 0.7 add_bitcast_fusion
  0.7 0.1 copy.7
  0.8 0.8 pad_add_fusion.3
  1.6 1.9 %collective-permute-start.1 = (s32[2,5]{1,0:T(2,128)S(1)}, s32[2,5]{1,0:T(2,128)S(1)}, u32[]{:S(2)}, u32[]{:S(2)}) collective-permute-start(s32[2,5]{1,0:T(2,128)S(1)} %pad_add_fusion.3), channel_id=1, source_target_pairs={{1,0},{2,1},{3,2},{4,3},{5,4},{6,5},{7,6},{8,7},{9,8},{10,9},{11,1... | collective-permute-start | bytes 128 | tf_op jit(solution)/shard_map/ppermute | solution.py:183
  3.5 3.5 %collective-permute-start = (s32[2,5]{1,0:T(2,128)S(1)}, s32[2,5]{1,0:T(2,128)S(1)}, u32[]{:S(2)}, u32[]{:S(2)}) collective-permute-start(s32[2,5]{1,0:T(2,128)S(1)} %pad_add_fusion.3), channel_id=1, source_target_pairs={{0,1},{1,2},{2,3},{3,4},{4,5},{5,6},{6,7},{7,8},{8,9},{9,10},{10,1... | collective-permute-start | bytes 128 | tf_op jit(solution)/shard_map/ppermute | solution.py:183
  7.0 3.5 %collective-permute-start.2 = (f32[2,4,128,128]{3,2,1,0:T(8,128)}, f32[2,4,128,128]{3,2,1,0:T(8,128)S(1)}, u32[]{:S(2)}, u32[]{:S(2)}) collective-permute-start(f32[2,4,128,128]{3,2,1,0:T(8,128)} %param.4), channel_id=1, source_target_pairs={{0,1},{1,2},{2,3},{3,4},{4,5},{5,6},{6,7},{7,8},{8,9},{9,10},{10,1... | collective-permute-start | bytes 1572872 | tf_op jit(solution)/shard_map/ppermute | solution.py:183
  10.6 9.3 %collective-permute-start.3 = (f32[2,4,128,128]{3,2,1,0:T(8,128)}, f32[2,4,128,128]{3,2,1,0:T(8,128)S(1)}, u32[]{:S(2)}, u32[]{:S(2)}) collective-permute-start(f32[2,4,128,128]{3,2,1,0:T(8,128)} %param.4), channel_id=1, source_target_pairs={{1,0},{2,1},{3,2},{4,3},{5,4},{6,5},{7,6},{8,7},{9,8},{10,9},{11,1... | collective-permute-start | bytes 1572872 | tf_op jit(solution)/shard_map/ppermute | solution.py:183
  20.4 0.8 pad_add_fusion.1
  21.2 0.1 slice_reduce_fusion
  21.4 0.1 copy.8
  21.5 0.1 select_reduce_fusion.1
  21.7 0.6 pad.4.pattern
  22.3 0.7 pad_add_fusion.2
  23.0 0.7 fusion.4
  23.7 5.8 %collective-permute-done.2 = f32[2,4,128,128]{3,2,1,0:T(8,128)S(1)} collective-permute-done((f32[2,4,128,128]{3,2,1,0:T(8,128)}, f32[2,4,128,128]{3,2,1,0:T(8,128)S(1)}, u32[]{:S(2)}, u32[]{:S(2)}) %collective-permute-start.2) | collective-permute-done | bytes 524320 | tf_op jit(solution)/shard_map/ppermute | solution.py:183
  29.5 12.2 %collective-permute-done.3 = f32[2,4,128,128]{3,2,1,0:T(8,128)S(1)} collective-permute-done((f32[2,4,128,128]{3,2,1,0:T(8,128)}, f32[2,4,128,128]{3,2,1,0:T(8,128)S(1)}, u32[]{:S(2)}, u32[]{:S(2)}) %collective-permute-start.3) | collective-permute-done | bytes 524320 | tf_op jit(solution)/shard_map/ppermute | solution.py:183
  41.8 5.0 %select_add_fusion.1 = f32[1,4,128,128]{3,2,1,0:T(8,128)S(1)} fusion(f32[2,4,128,128]{3,2,1,0:T(8,128)S(1)} %collective-permute-done.3, f32[2,4,128,128]{3,2,1,0:T(8,128)S(1)} %collective-permute-done.2, f32[2,4,128,128]{3,2,1,0:T(8,128)} %param.4, pred[]{:T(512)} %bitcast.12, pred[]{:T(512)} %bitcast.11, pred[]{:T(512)} %bitcast.10, pred[]{:T(512)} %bitcast.9, ...), kind=kLoop, calls=%fused_computation.2 | loop fusion | flops 720896 | bytes 1835014 | tf_op jit(solution)/shard_map/add | solution.py:201
  46.8 3.7 %select_add_fusion = f32[1,4,128,128]{3,2,1,0:T(8,128)S(1)} fusion(f32[2,4,128,128]{3,2,1,0:T(8,128)S(1)} %collective-permute-done.3, f32[2,4,128,128]{3,2,1,0:T(8,128)S(1)} %collective-permute-done.2, f32[2,4,128,128]{3,2,1,0:T(8,128)S(1)} %copy-done, pred[]{:T(512)} %bitcast.18, pred[]{:T(512)} %bitcast.17, pred[]{:T(512)} %bitcast.16, pred[]{:T(512)} %bitcast.15, ...), kind=kLoop, calls=%fused_computation.1 | loop fusion | flops 720896 | bytes 1835014 | tf_op jit(solution)/shard_map/add | solution.py:201
  50.5 0.8 pad_maximum_fusion
  51.3 70.8 %exchange.1 = (f32[4,8,128,128]{3,2,1,0:T(8,128)}, s32[4,8,128]{2,1,0:T(8,128)}) custom-call(f32[8,128,128]{2,1,0:T(8,128)} %bitcast.22, s32[8,128]{1,0:T(8,128)} %pad.4.pattern), custom_call_target="tpu_custom_call" | custom-call | tf_op jit(solution)/shard_map/exchange/pallas_call | solution.py:95
  122.1 0.7 slice.83
  123.0 0.4 select_reduce_fusion
  123.4 0.6 reshape.117.index
  124.0 5.0 %purify.1 = f32[2,4,128,128]{3,2,1,0:T(8,128)} custom-call(s32[64]{0:T(128)} %reshape.117.index, f32[8,128,128]{2,1,0:T(8,128)} %bitcast.23, f32[32,128,128]{2,1,0:T(8,128)} %bitcast.24), custom_call_target="tpu_custom_call" | custom-call | tf_op jit(solution)/shard_map/purify/pallas_call | solution.py:164
  (19 shorter events, 0.8 us)
Async XLA Ops:
  0.0 46.8 %copy-start = (f32[2,4,128,128]{3,2,1,0:T(8,128)S(1)}, f32[2,4,128,128]{3,2,1,0:T(8,128)}, u32[]{:S(2)}) copy-start(f32[2,4,128,128]{3,2,1,0:T(8,128)} %param.4) | copy-start | bytes 1572868
  1.6 18.8 %collective-permute-start.1 = (s32[2,5]{1,0:T(2,128)S(1)}, s32[2,5]{1,0:T(2,128)S(1)}, u32[]{:S(2)}, u32[]{:S(2)}) collective-permute-start(s32[2,5]{1,0:T(2,128)S(1)} %pad_add_fusion.3), channel_id=1, source_target_pairs={{1,0},{2,1},{3,2},{4,3},{5,4},{6,5},{7,6},{8,7},{9,8},{10,9},{11,1... | collective-permute-start | bytes 128 | tf_op jit(solution)/shard_map/ppermute | solution.py:183
  3.5 16.9 %collective-permute-start = (s32[2,5]{1,0:T(2,128)S(1)}, s32[2,5]{1,0:T(2,128)S(1)}, u32[]{:S(2)}, u32[]{:S(2)}) collective-permute-start(s32[2,5]{1,0:T(2,128)S(1)} %pad_add_fusion.3), channel_id=1, source_target_pairs={{0,1},{1,2},{2,3},{3,4},{4,5},{5,6},{6,7},{7,8},{8,9},{9,10},{10,1... | collective-permute-start | bytes 128 | tf_op jit(solution)/shard_map/ppermute | solution.py:183
  7.0 22.5 %collective-permute-start.2 = (f32[2,4,128,128]{3,2,1,0:T(8,128)}, f32[2,4,128,128]{3,2,1,0:T(8,128)S(1)}, u32[]{:S(2)}, u32[]{:S(2)}) collective-permute-start(f32[2,4,128,128]{3,2,1,0:T(8,128)} %param.4), channel_id=1, source_target_pairs={{0,1},{1,2},{2,3},{3,4},{4,5},{5,6},{6,7},{7,8},{8,9},{9,10},{10,1... | collective-permute-start | bytes 1572872 | tf_op jit(solution)/shard_map/ppermute | solution.py:183
  10.6 31.2 %collective-permute-start.3 = (f32[2,4,128,128]{3,2,1,0:T(8,128)}, f32[2,4,128,128]{3,2,1,0:T(8,128)S(1)}, u32[]{:S(2)}, u32[]{:S(2)}) collective-permute-start(f32[2,4,128,128]{3,2,1,0:T(8,128)} %param.4), channel_id=1, source_target_pairs={{1,0},{2,1},{3,2},{4,3},{5,4},{6,5},{7,6},{8,7},{9,8},{10,9},{11,1... | collective-permute-start | bytes 1572872 | tf_op jit(solution)/shard_map/ppermute | solution.py:183
  46.8 76.2 %copy-start.1 = (s32[2,4]{1,0:T(2,128)S(1)}, s32[2,4]{1,0:T(2,128)}, u32[]{:S(2)}) copy-start(s32[2,4]{1,0:T(2,128)} %param.7) | copy-start | bytes 100

commit v2 on v1

v2 whole, which is shorter than its diff:
```python
import functools

import jax
import jax.numpy as jnp
from jax import lax
from jax.experimental import pallas as pl
from jax.experimental.pallas import tpu as pltpu
from jax.sharding import PartitionSpec as P

MESH = pl.DeviceIdType.MESH
ROWS, SLOTS, ORDER = 2, 4, 128
CHUNKS = ROWS * SLOTS
Z_LO = 8


def place():
    slab, group = lax.axis_index("blk"), lax.axis_index("grp")
    return slab // 4, (slab // 2) % 2, slab % 2, group // Z_LO, group % Z_LO


M1, P1, P7, P9, FC, YN, YF, XC, XB, XA, SC, SB, SA, TC, TB, TA = range(16)
PLACES = 16


def exchange_kernel(blocks, labels, far, far_labels, send_sem, recv_sem):
    x, z_hi, core, y, z_lo = place()
    z = z_hi * Z_LO + z_lo

    def at(x_, z_, core_, y_):
        return ((x_ * 2 + z_ // Z_LO) * 2 + core_, y_ * Z_LO + z_ % Z_LO)

    def along_z(by):
        return at(x, (z + by + 2 * Z_LO) % (2 * Z_LO), core, y)

    inner_low = (z_lo + Z_LO - 1) // Z_LO
    edge_high = (z_lo + 1) // Z_LO
    edge_low = 1 - inner_low
    edge = edge_low + edge_high
    x_to = at((x + 5 - 2 * z_hi) % 4, z, core, y)
    x_from = at((x + 3 + 2 * z_hi) % 4, z, core, y)
    y_to = at(x, z, core, (y + 5 - 2 * edge_high) % 4)
    y_from = at(x, z, core, (y + 3 + 2 * edge_high) % 4)
    sibling = at(x, z, 1 - core, y)
    below, above = P7 + (YF - P7) * edge_low, P9 + (YF - P9) * edge_high

    barrier = pltpu.get_barrier_semaphore()
    peers = [along_z(by) for by in (1, -1, 6, -6)] + [x_to, x_from, y_to, y_from, sibling]
    for peer in peers:
        pl.semaphore_signal(barrier, inc=1, device_id=peer, device_id_type=MESH)
    pl.semaphore_wait(barrier, len(peers))

    def ref(place_, i):
        if place_ is None:
            return labels if i == CHUNKS else blocks.at[i]
        return far_labels.at[place_] if i == CHUNKS else far.at[place_, i]

    def copy(src, dst, i, peer):
        return pltpu.make_async_remote_copy(
            src_ref=ref(src, i),
            dst_ref=ref(dst, i),
            send_sem=send_sem.at[dst, i],
            recv_sem=recv_sem.at[dst, i],
            device_id=peer,
            device_id_type=MESH,
        )

    def send(src, dst, i, peer):
        copy(src, dst, i, peer).start()

    def arrived(dst, i):
        copy(dst, dst, i, sibling).wait_recv()

    def sent(dst, i):
        copy(dst, dst, i, sibling).wait_send()

    pieces = [CHUNKS] + [c for i in range(CHUNKS // 2) for c in (i, i + CHUNKS // 2)]
    upward = {i: i < CHUNKS // 2 or i == CHUNKS for i in pieces}

    for i in pieces:
        send(None, M1 if upward[i] else P1, i, along_z(1 if upward[i] else -1))
    for i in pieces:
        send(None, SC, i, sibling)
    for i in pieces:
        here = M1 if upward[i] else P1
        arrived(here, i)
        send(here, P9 if upward[i] else P7, i, along_z(6 if upward[i] else -6))
        send(None, P1 if upward[i] else M1, i, along_z(-1 if upward[i] else 1))

        @pl.when(edge_low == 1 if upward[i] else edge_high == 1)
        def _():
            send(here, YF, i, y_to)

    for i in pieces:
        here = P1 if upward[i] else M1
        arrived(here, i)

        @pl.when(edge_high == 1 if upward[i] else edge_low == 1)
        def _():
            send(here, YF, i, y_to)

    for i in pieces:
        @pl.when(edge_low == 0)
        def _():
            send(M1, SB, i, sibling)

        @pl.when(edge_high == 0)
        def _():
            send(P1, SA, i, sibling)

    for i in pieces:
        here = P9 if upward[i] else P7
        arrived(here, i)
        send(here, FC, i, along_z(1 if upward[i] else -1))

        @pl.when(edge == 1)
        def _():
            arrived(YF, i)

        if upward[i]:
            send(above, XA, i, x_to)
        else:
            send(below, XB, i, x_to)

        @pl.when(edge_high == 1 if upward[i] else edge_low == 1)
        def _():
            send(here, YN, i, y_to)

    for i in pieces:
        arrived(FC, i)
        send(FC, P7 if upward[i] else P9, i, along_z(1 if upward[i] else -1))
        send(FC, XC, i, x_to)

    crossed = (z_hi + core) % 2
    pass_center = FC + (XC - FC) * crossed
    pass_below = below + (XB - below) * crossed
    pass_above = above + (XA - above) * crossed
    for i in pieces:
        if upward[i]:
            arrived(XA, i)
            send(pass_above, TA, i, sibling)
        else:
            arrived(XB, i)
            send(pass_below, TB, i, sibling)

    for i in pieces:
        here = P7 if upward[i] else P9
        arrived(here, i)
        if upward[i]:
            send(below, XB, i, x_to)
        else:
            send(above, XA, i, x_to)

        @pl.when(edge_low == 1 if upward[i] else edge_high == 1)
        def _():
            send(here, YN, i, y_to)

    for i in pieces:
        arrived(XC, i)
        send(pass_center, TC, i, sibling)

    @pl.when(edge == 1)
    def _():
        for i in pieces:
            arrived(YN, i)

    for i in pieces:
        @pl.when(edge_low == 1)
        def _():
            send(YN, SB, i, sibling)

        @pl.when(edge_high == 1)
        def _():
            send(YN, SA, i, sibling)

    for i in pieces:
        if upward[i]:
            arrived(XB, i)
            send(pass_below, TB, i, sibling)
        else:
            arrived(XA, i)
            send(pass_above, TA, i, sibling)

    always = [p for p in range(PLACES) if p not in (YN, YF)]
    for i in pieces:
        for p in (SC, SB, SA, TC, TB, TA):
            arrived(p, i)
    for i in pieces:
        for p in always:
            sent(p, i)

    @pl.when(edge == 1)
    def _():
        for i in pieces:
            sent(YN, i)
            sent(YF, i)


def exchange(blocks, labels):
    vmem = pl.BlockSpec(memory_space=pltpu.VMEM)
    anywhere = pl.BlockSpec(memory_space=pl.ANY)
    return pl.pallas_call(
        exchange_kernel,
        out_shape=(
            jax.ShapeDtypeStruct((PLACES, CHUNKS, ORDER, ORDER), jnp.float32),
            jax.ShapeDtypeStruct((PLACES, 8, 128), jnp.int32),
        ),
        in_specs=[vmem, vmem],
        out_specs=(anywhere, anywhere),
        scratch_shapes=[
            pltpu.SemaphoreType.DMA((PLACES, CHUNKS + 1)),
            pltpu.SemaphoreType.DMA((PLACES, CHUNKS + 1)),
        ],
        compiler_params=pltpu.CompilerParams(collective_id=0, has_side_effects=True),
        name="exchange",
    )(blocks, labels)


PANEL = (1 + PLACES) * CHUNKS


def split(value):
    high = value.astype(jnp.bfloat16)
    return high, (value - high.astype(jnp.float32)).astype(jnp.bfloat16)


def dot3(left, right_high, right_low):
    high, low = split(left)
    dot = functools.partial(jnp.dot, preferred_element_type=jnp.float32)
    return dot(high, right_high) + (dot(high, right_low) + dot(low, right_high))


def purify_kernel(index, own, far, out, panel, right_high, right_low, sem):
    fetched = [
        pltpu.make_async_copy(far, panel.at[pl.ds(CHUNKS, PLACES * CHUNKS)], sem.at[0]),
        pltpu.make_async_copy(own, panel.at[pl.ds(0, CHUNKS)], sem.at[1]),
    ]
    for copy in fetched:
        copy.start()
    panel[PANEL] = jnp.zeros((ORDER, ORDER), jnp.float32)
    for copy in fetched:
        copy.wait()

    def product(stage, j, left):
        for a in range(SLOTS):
            for b in range(SLOTS):
                at = index[CHUNKS + ((stage * ROWS + j) * SLOTS + a) * SLOTS + b]
                rows, cols = pl.ds(a * ORDER, ORDER), pl.ds(b * ORDER, ORDER)
                high, low = split(panel[at])
                right_high[rows, cols] = high
                right_low[rows, cols] = low
        return dot3(left, right_high[...], right_low[...])

    for j in range(ROWS):
        left = jnp.concatenate([panel[index[j * SLOTS + a]] for a in range(SLOTS)], axis=1)
        square = product(0, j, left)
        cube = product(1, j, square)
        result = 3.0 * square - 2.0 * cube
        for b in range(SLOTS):
            out[j, b] = result[:, b * ORDER : (b + 1) * ORDER]


def purify(index, own, far):
    vmem = pl.BlockSpec(memory_space=pltpu.VMEM)
    anywhere = pl.BlockSpec(memory_space=pl.ANY)
    return pl.pallas_call(
        purify_kernel,
        out_shape=jax.ShapeDtypeStruct((ROWS, SLOTS, ORDER, ORDER), jnp.float32),
        in_specs=[pl.BlockSpec(memory_space=pltpu.SMEM), anywhere, anywhere],
        out_specs=vmem,
        scratch_shapes=[
            pltpu.VMEM((PANEL + 1, ORDER, ORDER), jnp.float32),
            pltpu.VMEM((SLOTS * ORDER, SLOTS * ORDER), jnp.bfloat16),
            pltpu.VMEM((SLOTS * ORDER, SLOTS * ORDER), jnp.bfloat16),
            pltpu.SemaphoreType.DMA((2,)),
        ],
        name="purify",
    )(index, own, far)


def per_device(blocks, columns, owner_map, targets):
    group_size = lax.axis_size("grp")
    slab, group = lax.axis_index("blk"), lax.axis_index("grp")
    _, _, _, _, z_lo = place()
    blocks = blocks.reshape(CHUNKS, ORDER, ORDER)
    labels = jnp.pad(
        jnp.concatenate([owner_map[:, None], columns], axis=1),
        ((0, 8 - ROWS), (0, 128 - SLOTS - 1)),
    )
    far, far_labels = exchange(blocks, labels)

    tiles = jnp.concatenate([labels[None], far_labels], axis=0)[:, :ROWS, : SLOTS + 1]
    tile = jnp.arange(1 + PLACES, dtype=jnp.int32)[:, None]
    unused = ((tile == 1 + YN) | (tile == 1 + YF)) & (z_lo > 0) & (z_lo < Z_LO - 1)
    owners = jnp.where(unused, -2, tiles[:, :, 0]).reshape(-1)
    cols = tiles[:, :, 1:].reshape(-1, SLOTS)
    own_ids = (slab * group_size + group) * ROWS + jnp.arange(ROWS, dtype=jnp.int32)
    mine = owners[None, :] == own_ids[:, None]
    local_cols = jnp.sum(jnp.where(mine[:, :, None], cols[None], 0), axis=1)
    first = jnp.arange(owners.shape[0], dtype=jnp.int32) * SLOTS
    left = jnp.sum(jnp.where(mine, first[None], 0), axis=1)[:, None]
    left = left + jnp.arange(SLOTS, dtype=jnp.int32)[None]

    left_ids = jnp.stack([local_cols, targets])
    found = (left_ids[:, :, :, None, None] == jnp.repeat(owners, SLOTS)) & (
        targets[None, :, None, :, None] == cols.reshape(-1)
    )
    right = jnp.min(jnp.where(found, jnp.arange(PANEL, dtype=jnp.int32), PANEL), axis=-1)
    index = jnp.concatenate([left.reshape(-1), right.reshape(-1)])
    return purify(index, blocks, far.reshape(PLACES * CHUNKS, ORDER, ORDER))


def solution(mesh):
    return jax.shard_map(
        per_device,
        mesh=mesh,
        in_specs=(
            P(("blk", "grp"), None, None, None),
            P(("blk", "grp"), None),
            P(("blk", "grp")),
            P(("blk", "grp"), None),
        ),
        out_specs=P(("blk", "grp"), None, None, None),
        check_vma=False,
    )
```

time: 129 us -> 117 us (0.907)
  the two profiles are of different devices: /device:TPU:49 before, /device:TPU:1 now
where the time goes in v2:
time: 117 us
  Pallas kernels  109 us (93%)
  other arithmetic  5.76 us (5%)
  local copies, waits for them, and re-layouts  2.17 us (2%)
    pallas_call x1, Pallas kernels, exchange(): pl.pallas_call(exchange_kernel, out_shape=(jax.ShapeDtypeStruct((PLACES,...  102 us
    pallas_call x1, Pallas kernels, purify(): pl.pallas_call(purify_kernel, out_shape=jax.ShapeDtypeStruct((ROWS, SLOTS...  6.81 us

profile of v2, /device:TPU:1, one launch (start us, length us, event | category | flops | bytes accessed | tf_op | source)
XLA Modules:
  0.0 116.8 jit_solution(11859676185902724217)
XLA Ops:
  0.0 0.7 copy.7
  0.8 0.8 pad_add_fusion.2
  1.5 0.1 broadcast_in_dim.73
  1.6 0.1 broadcast_in_dim.74
  1.7 0.6 pad_bitcast_fusion
  2.3 102.0 %exchange.1 = (f32[16,8,128,128]{3,2,1,0:T(8,128)}, s32[16,8,128]{2,1,0:T(8,128)}) custom-call(f32[8,128,128]{2,1,0:T(8,128)} %bitcast.8, s32[8,128]{1,0:T(8,128)} %get-tuple-element.12.labels), custom_call_target="tpu_custom_call" | custom-call | tf_op jit(solution)/shard_map/exchange/pallas_call | solution.py:201
  104.3 1.2 %add_reduce_fusion = s32[17,2]{1,0:T(8,128)S(1)} fusion(s32[16,8,128]{2,1,0:T(8,128)} %get-tuple-element.7, s32[1,8,128]{2,1,0:T(8,128)S(1)} %get-tuple-element.11), kind=kLoop, calls=%fused_computation.2 | loop fusion | flops 34 | bytes 69768 | tf_op jit(solution)/shard_map/slice | solution.py:294
  105.5 0.9 pad_add_fusion
  106.4 0.1 squeeze.3
  106.5 0.2 select_reduce_fusion.2
  106.7 0.1 iota_add_fusion
  106.8 0.1 add.43
  106.9 0.1 eq.85
  107.0 0.8 broadcast_compare_fusion.1
  107.8 0.1 copy.8
  107.9 0.1 select_reduce_fusion.1
  108.0 0.7 pad_add_fusion.1
  108.7 0.1 broadcast_in_dim.84
  108.8 0.1 eq.81
  108.9 0.1 broadcast_compare_fusion
  109.0 0.4 select_reduce_fusion
  109.3 0.1 reshape.96
  109.4 0.6 pad_add_fusion.3.index
  110.0 6.8 %purify.1 = f32[2,4,128,128]{3,2,1,0:T(8,128)} custom-call(s32[72]{0:T(128)} %pad_add_fusion.3.index, f32[8,128,128]{2,1,0:T(8,128)} %bitcast.9, f32[128,128,128]{2,1,0:T(8,128)} %bitcast.7), custom_call_target="tpu_custom_call" | custom-call | tf_op jit(solution)/shard_map/purify/pallas_call | solution.py:265
  (4 shorter events, 0.0 us)

commit v3 on v0

v3 whole, which is shorter than its diff:
```python
import functools

import jax
import jax.numpy as jnp
from jax import lax
from jax.experimental import pallas as pl
from jax.experimental.pallas import tpu as pltpu
from jax.sharding import PartitionSpec as P

MESH = pl.DeviceIdType.MESH
ROWS, SLOTS, ORDER = 2, 4, 128
CHUNKS = ROWS * SLOTS
Z_LO = 8


def place():
    slab, group = lax.axis_index("blk"), lax.axis_index("grp")
    return slab // 4, (slab // 2) % 2, slab % 2, group // Z_LO, group % Z_LO


M1, P1, P7, P9, FC, YN, YF, XC, XB, XA, SC, SB, SA, TC, TB, TA = range(16)
PLACES = 16


PANEL = (PLACES + 1) * CHUNKS
QUERIES = 2 * ROWS * SLOTS * SLOTS


def find(queries, known, index):
    owners = known[:, :CHUNKS, :].reshape(PANEL, 128)
    cols = known[:, CHUNKS:, :].reshape(PANEL, 128)
    at = lax.broadcasted_iota(jnp.int32, (PANEL, 128), 0)
    row, slot, wanted, target_row, stage = [queries[i : i + 1, :] for i in range(5)]
    mine = (owners == row) & (at % SLOTS == slot)
    left = jnp.min(jnp.where(mine, at, PANEL), axis=0, keepdims=True)
    column = jnp.sum(jnp.where(mine, cols, 0), axis=0, keepdims=True)
    middle = jnp.where(stage == 1, target_row, column)
    found = (owners == middle) & (cols == wanted)
    right = jnp.min(jnp.where(found, at, PANEL), axis=0, keepdims=True)
    lane = lax.broadcasted_iota(jnp.int32, (1, 128), 1)

    def scalar(vector, q):
        return jnp.sum(jnp.where(lane == q, vector, 0))

    for j in range(ROWS):
        for a in range(SLOTS):
            index[j * SLOTS + a] = scalar(left, (j * SLOTS + a) * SLOTS)
    for q in range(QUERIES):
        index[CHUNKS + q] = scalar(right, q)


def split(value):
    high = value.astype(jnp.bfloat16)
    return high, (value - high.astype(jnp.float32)).astype(jnp.bfloat16)


def dot3(left, right_high, right_low):
    high, low = split(left)
    dot = functools.partial(jnp.dot, preferred_element_type=jnp.float32)
    return dot(high, right_high) + (dot(high, right_low) + dot(low, right_high))


def kernel(
    queries, blocks, labels, out, panel, known, right_high, right_low, index, send_sem, recv_sem
):
    x, z_hi, core, y, z_lo = place()
    z = z_hi * Z_LO + z_lo

    def at(x_, z_, core_, y_):
        return ((x_ * 2 + z_ // Z_LO) * 2 + core_, y_ * Z_LO + z_ % Z_LO)

    def along_z(by):
        return at(x, (z + by + 2 * Z_LO) % (2 * Z_LO), core, y)

    inner_low = (z_lo + Z_LO - 1) // Z_LO
    edge_high = (z_lo + 1) // Z_LO
    edge_low = 1 - inner_low
    edge = edge_low + edge_high
    x_to = at((x + 5 - 2 * z_hi) % 4, z, core, y)
    x_from = at((x + 3 + 2 * z_hi) % 4, z, core, y)
    y_to = at(x, z, core, (y + 5 - 2 * edge_high) % 4)
    y_from = at(x, z, core, (y + 3 + 2 * edge_high) % 4)
    sibling = at(x, z, 1 - core, y)
    below, above = P7 + (YF - P7) * edge_low, P9 + (YF - P9) * edge_high

    for p in (YN, YF):
        known[p] = jnp.full(known.shape[1:], -2, jnp.int32)

    barrier = pltpu.get_barrier_semaphore()
    peers = [along_z(by) for by in (1, -1, 6, -6)] + [x_to, x_from, y_to, y_from, sibling]
    for peer in peers:
        pl.semaphore_signal(barrier, inc=1, device_id=peer, device_id_type=MESH)
    pl.semaphore_wait(barrier, len(peers))

    def ref(place_, i):
        if place_ is None:
            return labels if i == CHUNKS else blocks.at[i]
        return known.at[place_] if i == CHUNKS else panel.at[place_ * CHUNKS + i]

    def copy(src, dst, i, peer):
        return pltpu.make_async_remote_copy(
            src_ref=ref(src, i),
            dst_ref=ref(dst, i),
            send_sem=send_sem.at[dst, i],
            recv_sem=recv_sem.at[dst, i],
            device_id=peer,
            device_id_type=MESH,
        )

    def send(src, dst, i, peer):
        copy(src, dst, i, peer).start()

    def arrived(dst, i):
        copy(dst, dst, i, sibling).wait_recv()

    def sent(dst, i):
        copy(dst, dst, i, sibling).wait_send()

    half = CHUNKS // 2
    pieces = list(range(CHUNKS + 1))
    upward = {i: i < half or i == CHUNKS for i in pieces}

    def of(k):
        return ([CHUNKS] if k == 0 else []) + [k, k + half]

    def start(k):
        for i in of(k):
            send(None, M1 if upward[i] else P1, i, along_z(1 if upward[i] else -1))

    def six_on(k):
        for i in of(k):
            here = M1 if upward[i] else P1
            arrived(here, i)
            send(None, P1 if upward[i] else M1, i, along_z(-1 if upward[i] else 1))
            send(here, P9 if upward[i] else P7, i, along_z(6 if upward[i] else -6))

            @pl.when(edge_low == 1 if upward[i] else edge_high == 1)
            def _():
                send(here, YF, i, y_to)

    def other_way(k):
        for i in of(k):
            here = P1 if upward[i] else M1
            arrived(here, i)

            @pl.when(edge_high == 1 if upward[i] else edge_low == 1)
            def _():
                send(here, YF, i, y_to)

    def near():
        for i in pieces:
            @pl.when(edge_low == 0)
            def _():
                send(M1, SB, i, sibling)

            @pl.when(edge_high == 0)
            def _():
                send(P1, SA, i, sibling)

    def to_far(k):
        for i in of(k):
            here = P9 if upward[i] else P7
            arrived(here, i)
            send(here, FC, i, along_z(1 if upward[i] else -1))

            @pl.when(edge_high == 1 if upward[i] else edge_low == 1)
            def _():
                send(here, YN, i, y_to)

    def cross(k):
        for i in of(k):
            @pl.when(edge == 1)
            def _():
                arrived(YF, i)

            if upward[i]:
                send(above, XA, i, x_to)
            else:
                send(below, XB, i, x_to)

    def past_far(k):
        for i in of(k):
            arrived(FC, i)
            send(FC, P7 if upward[i] else P9, i, along_z(1 if upward[i] else -1))
            send(FC, XC, i, x_to)

    def end(k):
        for i in of(k):
            here = P7 if upward[i] else P9
            arrived(here, i)
            if upward[i]:
                send(below, XB, i, x_to)
            else:
                send(above, XA, i, x_to)

            @pl.when(edge_low == 1 if upward[i] else edge_high == 1)
            def _():
                send(here, YN, i, y_to)

    crossed = (z_hi + core) % 2
    pass_center = FC + (XC - FC) * crossed
    pass_below = below + (XB - below) * crossed
    pass_above = above + (XA - above) * crossed

    def pass_on(k, early):
        for i in of(k):
            if upward[i] == early:
                arrived(XA, i)
                send(pass_above, TA, i, sibling)
            else:
                arrived(XB, i)
                send(pass_below, TB, i, sibling)

    def pass_far(k):
        for i in of(k):
            arrived(XC, i)
            send(pass_center, TC, i, sibling)

    def near_end(which):
        @pl.when(edge_low == 1)
        def _():
            for i in which:
                arrived(YN, i)
                send(YN, SB, i, sibling)

        @pl.when(edge_high == 1)
        def _():
            for i in which:
                arrived(YN, i)
                send(YN, SA, i, sibling)

    for k in range(half):
        start(k)
    for i in [CHUNKS] + pieces[:-1]:
        send(None, SC, i, sibling)
    own = PLACES * CHUNKS
    for i in range(CHUNKS):
        panel[own + i] = blocks[i]
    panel[PANEL] = jnp.zeros((ORDER, ORDER), jnp.float32)
    known[PLACES] = labels[...]

    six_on(0), six_on(1)
    other_way(0), to_far(0), six_on(2), cross(0)
    other_way(1), to_far(1), six_on(3), past_far(0), cross(1)
    other_way(2), to_far(2), past_far(1), end(0), cross(2)
    other_way(3), near()
    pass_on(0, True), pass_on(1, True)
    to_far(3), past_far(2), end(1), cross(3)
    pass_far(0), pass_on(2, True), pass_on(0, False), near_end([CHUNKS])
    past_far(3), end(2)
    pass_far(1), pass_far(2), pass_on(3, True), pass_on(1, False)
    end(3)
    near_end(pieces[:-1])

    core_places = (SC, SB, SA, TC, TB, TA)
    for p in core_places:
        arrived(p, CHUNKS)
    find(queries, known, index)

    pass_on(2, False), pass_far(3), pass_on(3, False)
    for i in pieces[:-1]:
        for p in core_places:
            arrived(p, i)

    def product(stage, j, left):
        for a in range(SLOTS):
            for b in range(SLOTS):
                at_ = index[CHUNKS + ((stage * ROWS + j) * SLOTS + a) * SLOTS + b]
                rows, cols = pl.ds(a * ORDER, ORDER), pl.ds(b * ORDER, ORDER)
                high, low = split(panel[at_])
                right_high[rows, cols] = high
                right_low[rows, cols] = low
        return dot3(left, right_high[...], right_low[...])

    for j in range(ROWS):
        left = jnp.concatenate([panel[index[j * SLOTS + a]] for a in range(SLOTS)], axis=1)
        square = product(0, j, left)
        cube = product(1, j, square)
        result = 3.0 * square - 2.0 * cube
        for b in range(SLOTS):
            out[j, b] = result[:, b * ORDER : (b + 1) * ORDER]

    always = [p for p in range(PLACES) if p not in (YN, YF)]
    for i in pieces:
        for p in always:
            sent(p, i)

    @pl.when(edge == 1)
    def _():
        for i in pieces:
            sent(YN, i)
            sent(YF, i)


def per_device(blocks, columns, owner_map, targets):
    slab, group = lax.axis_index("blk"), lax.axis_index("grp")
    first_row = (slab * lax.axis_size("grp") + group) * ROWS

    def lanes(values):
        return jnp.broadcast_to(values.reshape(-1, 1), (CHUNKS, 128))

    labels = jnp.concatenate([lanes(jnp.repeat(owner_map, SLOTS)), lanes(columns)], axis=0)
    shape = (2, ROWS, SLOTS, SLOTS)
    stage, row, slot, _ = [lax.broadcasted_iota(jnp.int32, shape, i) for i in range(4)]
    queries = jnp.stack(
        [
            first_row + row,
            slot,
            jnp.broadcast_to(targets[None, :, None, :], shape),
            jnp.broadcast_to(targets[None, :, :, None], shape),
            stage,
        ]
    ).reshape(5, QUERIES)
    queries = jnp.pad(queries, ((0, 3), (0, 128 - QUERIES)), constant_values=-3)
    vmem = pl.BlockSpec(memory_space=pltpu.VMEM)
    return pl.pallas_call(
        kernel,
        out_shape=jax.ShapeDtypeStruct((ROWS, SLOTS, ORDER, ORDER), jnp.float32),
        in_specs=[vmem, vmem, vmem],
        out_specs=vmem,
        scratch_shapes=[
            pltpu.VMEM((PANEL + 1, ORDER, ORDER), jnp.float32),
            pltpu.VMEM((PLACES + 1, 2 * CHUNKS, 128), jnp.int32),
            pltpu.VMEM((SLOTS * ORDER, SLOTS * ORDER), jnp.bfloat16),
            pltpu.VMEM((SLOTS * ORDER, SLOTS * ORDER), jnp.bfloat16),
            pltpu.SMEM((CHUNKS + QUERIES,), jnp.int32),
            pltpu.SemaphoreType.DMA((PLACES, CHUNKS + 1)),
            pltpu.SemaphoreType.DMA((PLACES, CHUNKS + 1)),
        ],
        compiler_params=pltpu.CompilerParams(collective_id=0, has_side_effects=True),
        name="purify",
    )(queries, blocks.reshape(CHUNKS, ORDER, ORDER), labels)


def solution(mesh):
    return jax.shard_map(
        per_device,
        mesh=mesh,
        in_specs=(
            P(("blk", "grp"), None, None, None),
            P(("blk", "grp"), None),
            P(("blk", "grp")),
            P(("blk", "grp"), None),
        ),
        out_specs=P(("blk", "grp"), None, None, None),
        check_vma=False,
    )
```

time: 298 us -> 106 us (0.36)
  the two profiles are of different devices: /device:TPU:8 before, /device:TPU:1 now
where the time goes in v3:
time: 106 us
  Pallas kernels  100 us (94%)
  local copies, waits for them, and re-layouts  5.57 us (5%)
    pallas_call x1, Pallas kernels, per_device(): pl.pallas_call(kernel, out_shape=jax.ShapeDtypeStruct((ROWS, SLOTS, ORDER...  100 us
    unnamed x11, local copies, waits for them, and re-layouts  3.96 us

profile of v3, /device:TPU:1, one launch (start us, length us, event | category | flops | bytes accessed | tf_op | source)
XLA Modules:
  0.0 106.0 jit_solution(819928019604177398)
XLA Ops:
  0.0 0.0 copy-start.1
  0.0 0.7 copy-done.1
  0.7 0.0 copy-start.2
  0.7 0.1 reshape.22
  0.8 0.6 copy-done.2
  1.3 0.1 broadcast_in_dim.19
  1.4 0.1 reshape.21
  1.5 0.1 pad_add_fusion
  1.6 0.7 broadcast.11.labels
  2.2 0.1 constant_dynamic-update-slice_fusion.4
  2.3 0.0 copy-start
  2.3 0.7 copy-done
  3.0 0.1 constant_dynamic-update-slice_fusion.1
  3.1 0.1 reshape.19
  3.2 0.6 pad.4.queries
  3.8 100.3 %purify.1 = f32[2,4,128,128]{3,2,1,0:T(8,128)} custom-call(s32[8,128]{1,0:T(8,128)} %pad.4.queries, f32[8,128,128]{2,1,0:T(8,128)} %bitcast.1, s32[16,128]{1,0:T(8,128)} %broadcast.11.labels), custom_call_target="tpu_custom_call" | custom-call | tf_op jit(solution)/shard_map/purify/pallas_call | solution.py:316
  104.1 1.9 %copy.10 = f32[2,4,128,128]{3,2,1,0:T(8,128)} copy(f32[2,4,128,128]{3,2,1,0:T(8,128)} %purify.1) | data formatting | bytes 1048576
  (4 shorter events, 0.0 us)
Async XLA Ops:
  0.0 0.7 copy-start.1
  0.7 0.7 copy-start.2
  2.3 0.7 copy-start

commit v4 on v3

--- a/solution.py
+++ b/solution.py
@@ -10,6 +10,9 @@
 MESH = pl.DeviceIdType.MESH
 ROWS, SLOTS, ORDER = 2, 4, 128
 CHUNKS = ROWS * SLOTS
+PARTS = 2
+PIECES = CHUNKS * PARTS
+AHEAD = 2
 Z_LO = 8
 
 
@@ -92,10 +95,13 @@
         pl.semaphore_signal(barrier, inc=1, device_id=peer, device_id_type=MESH)
     pl.semaphore_wait(barrier, len(peers))
 
+    def part(i):
+        return pl.ds(i % PARTS * (ORDER // PARTS), ORDER // PARTS)
+
     def ref(place_, i):
         if place_ is None:
-            return labels if i == CHUNKS else blocks.at[i]
-        return known.at[place_] if i == CHUNKS else panel.at[place_ * CHUNKS + i]
+            return labels if i == PIECES else blocks.at[i // PARTS, part(i)]
+        return known.at[place_] if i == PIECES else panel.at[place_ * CHUNKS + i // PARTS, part(i)]
 
     def copy(src, dst, i, peer):
         return pltpu.make_async_remote_copy(
@@ -116,12 +122,12 @@
     def sent(dst, i):
         copy(dst, dst, i, sibling).wait_send()
 
-    half = CHUNKS // 2
-    pieces = list(range(CHUNKS + 1))
-    upward = {i: i < half or i == CHUNKS for i in pieces}
+    steps = PIECES // 2
+    pieces = list(range(PIECES + 1))
+    upward = {i: i < steps or i == PIECES for i in pieces}
 
     def of(k):
-        return ([CHUNKS] if k == 0 else []) + [k, k + half]
+        return ([PIECES] if k == 0 else []) + [k, k + steps]
 
     def start(k):
         for i in of(k):
@@ -147,8 +153,8 @@
             def _():
                 send(here, YF, i, y_to)
 
-    def near():
-        for i in pieces:
+    def near(k):
+        for i in of(k):
             @pl.when(edge_low == 0)
             def _():
                 send(M1, SB, i, sibling)
@@ -229,35 +235,40 @@
                 arrived(YN, i)
                 send(YN, SA, i, sibling)
 
-    for k in range(half):
+    for k in range(steps):
         start(k)
-    for i in [CHUNKS] + pieces[:-1]:
-        send(None, SC, i, sibling)
+    for k in range(steps):
+        for i in of(k):
+            send(None, SC, i, sibling)
     own = PLACES * CHUNKS
     for i in range(CHUNKS):
         panel[own + i] = blocks[i]
     panel[PANEL] = jnp.zeros((ORDER, ORDER), jnp.float32)
     known[PLACES] = labels[...]
 
-    six_on(0), six_on(1)
-    other_way(0), to_far(0), six_on(2), cross(0)
-    other_way(1), to_far(1), six_on(3), past_far(0), cross(1)
-    other_way(2), to_far(2), past_far(1), end(0), cross(2)
-    other_way(3), near()
-    pass_on(0, True), pass_on(1, True)
-    to_far(3), past_far(2), end(1), cross(3)
-    pass_far(0), pass_on(2, True), pass_on(0, False), near_end([CHUNKS])
-    past_far(3), end(2)
-    pass_far(1), pass_far(2), pass_on(3, True), pass_on(1, False)
-    end(3)
-    near_end(pieces[:-1])
+    def at_step(k, work):
+        if 0 <= k < steps:
+            work(k)
 
     core_places = (SC, SB, SA, TC, TB, TA)
-    for p in core_places:
-        arrived(p, CHUNKS)
-    find(queries, known, index)
-
-    pass_on(2, False), pass_far(3), pass_on(3, False)
+    for k in range(AHEAD):
+        six_on(k)
+    for k in range(steps + 4):
+        at_step(k, other_way)
+        at_step(k, to_far)
+        at_step(k + AHEAD, six_on)
+        at_step(k - 1, past_far)
+        at_step(k, cross)
+        at_step(k - 2, end)
+        at_step(k, near)
+        at_step(k - 2, lambda k: pass_on(k, True))
+        at_step(k - 3, pass_far)
+        at_step(k - 4, lambda k: near_end(of(k)))
+        at_step(k - 4, lambda k: pass_on(k, False))
+        if k == steps + 1:
+            for p in core_places:
+                arrived(p, PIECES)
+            find(queries, known, index)
     for i in pieces[:-1]:
         for p in core_places:
             arrived(p, i)
@@ -324,8 +335,8 @@
             pltpu.VMEM((SLOTS * ORDER, SLOTS * ORDER), jnp.bfloat16),
             pltpu.VMEM((SLOTS * ORDER, SLOTS * ORDER), jnp.bfloat16),
             pltpu.SMEM((CHUNKS + QUERIES,), jnp.int32),
-            pltpu.SemaphoreType.DMA((PLACES, CHUNKS + 1)),
-            pltpu.SemaphoreType.DMA((PLACES, CHUNKS + 1)),
+            pltpu.SemaphoreType.DMA((PLACES, PIECES + 1)),
+            pltpu.SemaphoreType.DMA((PLACES, PIECES + 1)),
         ],
         compiler_params=pltpu.CompilerParams(collective_id=0, has_side_effects=True),
         name="purify",

time: 106 us -> 101 us (0.953)
  Pallas kernels: 100 us -> 95.1 us
    pallas_call x1, Pallas kernels: 100 us -> 95.1 us  [per_device(): pl.pallas_call(kernel, out_shape=jax.ShapeDtypeStruct((ROWS, SLOTS, ORDER...]
where the time goes in v4:
time: 101 us
  Pallas kernels  95.1 us (94%)
  local copies, waits for them, and re-layouts  5.57 us (6%)
    pallas_call x1, Pallas kernels, per_device(): pl.pallas_call(kernel, out_shape=jax.ShapeDtypeStruct((ROWS, SLOTS, ORDER...  95.1 us
    unnamed x11, local copies, waits for them, and re-layouts  3.96 us

profile of v4, /device:TPU:1, one launch (start us, length us, event | category | flops | bytes accessed | tf_op | source)
XLA Modules:
  0.0 100.7 jit_solution(5088317425436627479)
XLA Ops:
  0.0 0.0 copy-start.1
  0.0 0.7 copy-done.1
  0.7 0.0 copy-start.2
  0.7 0.1 reshape.22
  0.8 0.6 copy-done.2
  1.3 0.1 broadcast_in_dim.19
  1.4 0.1 reshape.21
  1.5 0.1 pad_add_fusion
  1.6 0.7 broadcast.11.labels
  2.2 0.1 constant_dynamic-update-slice_fusion.4
  2.3 0.0 copy-start
  2.3 0.7 copy-done
  3.0 0.1 constant_dynamic-update-slice_fusion.1
  3.1 0.1 reshape.19
  3.2 0.6 pad.4.queries
  3.8 95.1 %purify.1 = f32[2,4,128,128]{3,2,1,0:T(8,128)} custom-call(s32[8,128]{1,0:T(8,128)} %pad.4.queries, f32[8,128,128]{2,1,0:T(8,128)} %bitcast.1, s32[16,128]{1,0:T(8,128)} %broadcast.11.labels), custom_call_target="tpu_custom_call" | custom-call | tf_op jit(solution)/shard_map/purify/pallas_call | solution.py:327
  98.9 1.9 %copy.10 = f32[2,4,128,128]{3,2,1,0:T(8,128)} copy(f32[2,4,128,128]{3,2,1,0:T(8,128)} %purify.1) | data formatting | bytes 1048576
  (4 shorter events, 0.0 us)
Async XLA Ops:
  0.0 0.7 copy-start.1
  0.7 0.7 copy-start.2
  2.3 0.7 copy-start

commit v5 on v4

--- a/solution.py
+++ b/solution.py
@@ -29,18 +29,26 @@
 QUERIES = 2 * ROWS * SLOTS * SLOTS
 
 
-def find(queries, known, index):
+def find(targets, known, index):
     owners = known[:, :CHUNKS, :].reshape(PANEL, 128)
     cols = known[:, CHUNKS:, :].reshape(PANEL, 128)
     at = lax.broadcasted_iota(jnp.int32, (PANEL, 128), 0)
-    row, slot, wanted, target_row, stage = [queries[i : i + 1, :] for i in range(5)]
+    lane = lax.broadcasted_iota(jnp.int32, (1, 128), 1)
+    slot, b = lane // SLOTS % SLOTS, lane % SLOTS
+    j, stage = lane // SLOTS**2 % ROWS, lane // (SLOTS**2 * ROWS)
+    first = (lax.axis_index("blk") * lax.axis_size("grp") + lax.axis_index("grp")) * ROWS
+    row = first + j
+    wanted = target_row = jnp.full((1, 128), -3, jnp.int32)
+    for r in range(ROWS):
+        for t in range(SLOTS):
+            wanted = jnp.where((j == r) & (b == t), targets[r, t], wanted)
+            target_row = jnp.where((j == r) & (slot == t), targets[r, t], target_row)
     mine = (owners == row) & (at % SLOTS == slot)
     left = jnp.min(jnp.where(mine, at, PANEL), axis=0, keepdims=True)
     column = jnp.sum(jnp.where(mine, cols, 0), axis=0, keepdims=True)
     middle = jnp.where(stage == 1, target_row, column)
     found = (owners == middle) & (cols == wanted)
     right = jnp.min(jnp.where(found, at, PANEL), axis=0, keepdims=True)
-    lane = lax.broadcasted_iota(jnp.int32, (1, 128), 1)
 
     def scalar(vector, q):
         return jnp.sum(jnp.where(lane == q, vector, 0))
@@ -64,7 +72,7 @@
 
 
 def kernel(
-    queries, blocks, labels, out, panel, known, right_high, right_low, index, send_sem, recv_sem
+    targets, blocks, labels, out, panel, known, right_high, right_low, index, send_sem, recv_sem, own_sem
 ):
     x, z_hi, core, y, z_lo = place()
     z = z_hi * Z_LO + z_lo
@@ -241,8 +249,8 @@
         for i in of(k):
             send(None, SC, i, sibling)
     own = PLACES * CHUNKS
-    for i in range(CHUNKS):
-        panel[own + i] = blocks[i]
+    mine = pltpu.make_async_copy(blocks, panel.at[pl.ds(own, CHUNKS)], own_sem)
+    mine.start()
     panel[PANEL] = jnp.zeros((ORDER, ORDER), jnp.float32)
     known[PLACES] = labels[...]
 
@@ -256,8 +264,8 @@
     for k in range(steps + 4):
         at_step(k, other_way)
         at_step(k, to_far)
+        at_step(k - 1, past_far)
         at_step(k + AHEAD, six_on)
-        at_step(k - 1, past_far)
         at_step(k, cross)
         at_step(k - 2, end)
         at_step(k, near)
@@ -268,10 +276,12 @@
         if k == steps + 1:
             for p in core_places:
                 arrived(p, PIECES)
-            find(queries, known, index)
+            find(targets, known, index)
     for i in pieces[:-1]:
         for p in core_places:
             arrived(p, i)
+
+    mine.wait()
 
     def product(stage, j, left):
         for a in range(SLOTS):
@@ -304,30 +314,19 @@
 
 
 def per_device(blocks, columns, owner_map, targets):
-    slab, group = lax.axis_index("blk"), lax.axis_index("grp")
-    first_row = (slab * lax.axis_size("grp") + group) * ROWS
-
     def lanes(values):
         return jnp.broadcast_to(values.reshape(-1, 1), (CHUNKS, 128))
 
     labels = jnp.concatenate([lanes(jnp.repeat(owner_map, SLOTS)), lanes(columns)], axis=0)
-    shape = (2, ROWS, SLOTS, SLOTS)
-    stage, row, slot, _ = [lax.broadcasted_iota(jnp.int32, shape, i) for i in range(4)]
-    queries = jnp.stack(
-        [
-            first_row + row,
-            slot,
-            jnp.broadcast_to(targets[None, :, None, :], shape),
-            jnp.broadcast_to(targets[None, :, :, None], shape),
-            stage,
-        ]
-    ).reshape(5, QUERIES)
-    queries = jnp.pad(queries, ((0, 3), (0, 128 - QUERIES)), constant_values=-3)
     vmem = pl.BlockSpec(memory_space=pltpu.VMEM)
     return pl.pallas_call(
         kernel,
         out_shape=jax.ShapeDtypeStruct((ROWS, SLOTS, ORDER, ORDER), jnp.float32),
-        in_specs=[vmem, vmem, vmem],
+        in_specs=[
+            pl.BlockSpec(memory_space=pltpu.SMEM),
+            pl.BlockSpec(memory_space=pl.ANY),
+            vmem,
+        ],
         out_specs=vmem,
         scratch_shapes=[
             pltpu.VMEM((PANEL + 1, ORDER, ORDER), jnp.float32),
@@ -337,10 +336,11 @@
             pltpu.SMEM((CHUNKS + QUERIES,), jnp.int32),
             pltpu.SemaphoreType.DMA((PLACES, PIECES + 1)),
             pltpu.SemaphoreType.DMA((PLACES, PIECES + 1)),
+            pltpu.SemaphoreType.DMA,
         ],
         compiler_params=pltpu.CompilerParams(collective_id=0, has_side_effects=True),
         name="purify",
-    )(queries, blocks.reshape(CHUNKS, ORDER, ORDER), labels)
+    )(targets, blocks.reshape(CHUNKS, ORDER, ORDER), labels)
 
 
 def solution(mesh):

time: 101 us -> 98.7 us (0.977)
  local copies, waits for them, and re-layouts: 5.57 us -> 4.03 us
    unnamed x11 -> x5, local copies, waits for them, and re-layouts: 3.96 us -> 3.12 us
where the time goes in v5:
time: 98.7 us; the launch traced here: 98.4 us
  Pallas kernels  94.3 us (96%)
  local copies, waits for them, and re-layouts  4.03 us (4%)
    pallas_call x1, Pallas kernels, per_device(): pl.pallas_call(kernel, out_shape=jax.ShapeDtypeStruct((ROWS, SLOTS, ORDER...  94.3 us
    unnamed x5, local copies, waits for them, and re-layouts  3.12 us

profile of v5, /device:TPU:1, one launch (start us, length us, event | category | flops | bytes accessed | tf_op | source)
XLA Modules:
  0.0 98.4 jit_solution(8415453604592957193)
XLA Ops:
  0.0 0.0 copy-start
  0.0 0.7 copy-done
  0.7 0.0 copy-start.1
  0.7 0.1 reshape.8
  0.8 0.6 copy-done.1
  1.3 0.1 broadcast_in_dim.17
  1.4 0.1 reshape.7
  1.5 0.1 pad_add_fusion
  1.6 0.7 broadcast.2.labels
  2.2 94.3 %purify.1 = f32[2,4,128,128]{3,2,1,0:T(8,128)} custom-call(s32[2,4]{1,0:T(2,128)} %targets.1, f32[8,128,128]{2,1,0:T(8,128)} %bitcast.1, s32[16,128]{1,0:T(8,128)} %broadcast.2.labels), custom_call_target="tpu_custom_call" | custom-call | tf_op jit(solution)/shard_map/purify/pallas_call | solution.py:322
  96.6 1.9 %copy.6 = f32[2,4,128,128]{3,2,1,0:T(8,128)} copy(f32[2,4,128,128]{3,2,1,0:T(8,128)} %purify.1) | data formatting | bytes 1048576
Async XLA Ops:
  0.0 0.7 copy-start
  0.7 0.7 copy-start.1
